TPU v7x, 512 devices: a whole 4x4x16 slice. The times are simulated.
512 devices in a mesh: seq: 64 (over z, y), exp: 8 (over x, core).
Axes of the slice: x: 4, y: 4, z: 16, core: 2. Of those that a mesh axis runs over, the one named last changes fastest.
Arguments:
- x_in: bfloat16 [4096, 8192], P('seq', 'exp'), may hold values from -6 to 6
- z_gate: bfloat16 [4096, 8192], P('seq', 'exp'), may hold values from -6 to 6
- dt_low: bfloat16 [4096, 256], P('seq'), may hold values from -6 to 6
- dt_weight: bfloat16 [256, 8192], P(None, 'exp'), may hold values from -0.375 to 0.375
- dt_bias: float32 [8192], P('exp'), may hold values from -9 to -1
- a_log: float32 [16, 8192], P(None, 'exp'), may hold values from -4 to 0
- conv_weight: float32 [4, 8192], P(None, 'exp'), may hold values from -3 to 3
- conv_bias: float32 [8192], P('exp'), may hold values from -0.5 to 0.5
- d_skip: float32 [8192], P('exp'), may hold values from 0.5 to 1.5
- b_and_c: float32 [2, 16, 4096], P(None, None, 'seq'), may hold values from -6 to 6
- hidden: bfloat16 [4096, 4096], P('seq', 'exp'), may hold values from -6 to 6
- router: bfloat16 [4096, 8], P('exp'), may hold values from -0.09375 to 0.09375
- expert_ids: int32 [4096, 2], P('seq'), may hold values from 0 to 7, all different within a row; in each aligned block of 64 rows (0 to 63, 64 to 127, ...) at most 18 rows name the same one
- w_gate: bfloat16 [4096, 98304], P('exp', 'seq'), may hold values from -0.09375 to 0.09375
- w_down: bfloat16 [98304, 4096], P('seq', 'exp'), may hold values from -0.0546875 to 0.0546875
Outputs:
- mamba_out: bfloat16 [4096, 8192], P('seq', 'exp')
- moe_out: bfloat16 [4096, 4096], P('seq', 'exp')
Inputs may be any that keep to these rules, and one draw needn't show every extreme that they name: `expert_ids`: each token names 2 different experts; among the 64 tokens of one block no expert is named more than 18 times, a bound that some expert reaches in every block.
All inputs are finite; a program needn't handle non-finite values.
Results may differ from a plain program's by a relative error of at most 0.018.
Values may be sent and summed in bfloat16 or wider, within the bound.
A program may use at most 128 MiB of HBM per device.

v0:
```python
import jax
import jax.numpy as jnp
from jax import lax
from jax.sharding import PartitionSpec as P

CAP = 18


def passed_along(value, axis, steps):
    count = lax.axis_size(axis)
    first, last = (max(0, -steps), min(count, count - steps))
    return lax.ppermute(value, axis, [(source, source + steps) for source in range(first, last)])


def carried_in(array, axis, join, neutral):
    place = lax.axis_index(axis)
    gathered = jax.tree.map(
        lambda a, kind: lax.all_gather(a.astype(kind), axis), array, (jnp.bfloat16, jnp.bfloat16)
    )
    state = jax.tree.map(lambda a, e: jnp.zeros_like(a) + jnp.asarray(e, a.dtype), array, neutral)

    def one(lap, state):
        return join(
            state,
            jax.tree.map(
                lambda a, own: lax.dynamic_index_in_dim(a, lap, 0, False).astype(own.dtype),
                gathered,
                array,
            ),
        )

    return lax.fori_loop(0, place, one, state)


def link_pairs(earlier, later):
    return (earlier[0] * later[0], later[0] * earlier[1] + later[1])


def mixer_scan(delta, activated, b_rows, c_rows, rates, start_state):
    token_count, channels = delta.shape
    block_len = 16
    block_count = token_count // block_len

    def regroup(values):
        return values.reshape((block_count, block_len) + values.shape[1:])

    def advance(carry, inputs):
        running, product = carry
        step_delta, step_x, step_b, step_c = inputs
        reads = []
        for position in range(block_len):
            factor = jnp.exp(step_delta[position][None, :] * rates)
            running = (
                factor * running
                + step_b[position][:, None] * (step_delta[position] * step_x[position])[None, :]
            )
            product = factor * product
            reads.append(jnp.sum(step_c[position][:, None] * running, axis=0))
        return ((running, product), (jnp.stack(reads),))

    initial = (start_state, jnp.ones(rates.shape, jnp.float32))
    finals, outputs = lax.scan(
        advance, initial, (regroup(delta), regroup(activated), regroup(b_rows), regroup(c_rows))
    )
    readout = outputs[0].reshape(token_count, channels)
    weighted_all = None
    return (readout, weighted_all, finals[0], finals[1])


def local(
    x_in,
    z_gate,
    dt_low,
    dt_weight,
    dt_bias,
    a_log,
    conv_weight,
    conv_bias,
    d_skip,
    b_and_c,
    hidden,
    router,
    expert_ids,
    w_gate,
    w_down,
):
    tok_rows = x_in.shape[0]
    kernel_taps = conv_weight.shape[0]
    edge_rows = passed_along(x_in[tok_rows - (kernel_taps - 1) :], "seq", 1)
    padded = jnp.concatenate([edge_rows, x_in], axis=0).astype(jnp.float32)
    convolved = jnp.zeros(x_in.shape, jnp.float32) + conv_bias[None, :]
    for offset in range(kernel_taps):
        convolved = convolved + conv_weight[offset][None, :] * padded[offset : offset + tok_rows]
    activated = jax.nn.silu(convolved)
    delta = jax.nn.softplus(
        jnp.dot(dt_low, dt_weight, preferred_element_type=jnp.float32) + dt_bias[None, :]
    )
    rates = -jnp.exp(a_log)
    b_rows = b_and_c[0].T
    c_rows = b_and_c[1].T
    zero_state = jnp.zeros(rates.shape, jnp.float32)
    readout, weighted_all, end_state, end_product = mixer_scan(
        delta, activated, b_rows, c_rows, rates, zero_state
    )
    identity = (jnp.ones(rates.shape, jnp.float32), jnp.zeros(rates.shape, jnp.float32))
    carried = carried_in((end_product, end_state), "seq", link_pairs, identity)
    entering = carried[1]
    readout = mixer_scan(delta, activated, b_rows, c_rows, rates, entering)[0]
    mamba_out = (
        (readout + d_skip[None, :] * activated) * jax.nn.silu(z_gate.astype(jnp.float32))
    ).astype(jnp.bfloat16)
    experts = router.shape[1]
    picks = expert_ids.shape[1]
    feature_width = hidden.shape[1]
    group_size = lax.axis_size("seq") // experts
    logits = lax.psum(jnp.dot(hidden, router, preferred_element_type=jnp.float32), "exp")
    expert_iota = lax.broadcasted_iota(jnp.int32, (1, 1, experts), 2)
    chosen = expert_ids[:, :, None] == expert_iota
    picked = jnp.sum(jnp.where(chosen, logits[:, None, :], 0.0), axis=2)
    gates = jax.nn.sigmoid(picked - picked[:, ::-1])
    flat_hits = chosen.reshape(tok_rows * picks, experts).astype(jnp.int32)
    earlier_hits = jnp.cumsum(flat_hits, axis=0) - flat_hits
    slots = jnp.sum(earlier_hits * flat_hits, axis=1).reshape(tok_rows, picks)
    slot_keys = expert_ids * CAP + slots
    slot_iota = lax.broadcasted_iota(jnp.int32, (experts * CAP, 1, 1), 0)
    matches = slot_keys[None] == slot_iota
    selector = jnp.sum(matches.astype(jnp.float32), axis=2).astype(jnp.bfloat16)
    blending = jnp.sum(jnp.where(matches, gates[None], 0.0), axis=2)
    packed = jnp.dot(selector, hidden, preferred_element_type=jnp.float32).astype(jnp.bfloat16)
    outgoing = jnp.broadcast_to(
        packed.reshape(experts, 1, CAP, feature_width), (experts, group_size, CAP, feature_width)
    )
    outgoing = outgoing.reshape(experts * group_size, CAP, feature_width)
    arrived = lax.all_to_all(outgoing, "seq", split_axis=0, concat_axis=0, tiled=True)
    sources, entries, features = arrived.shape
    routed = arrived.reshape(sources * entries, features)
    partial_value = jnp.dot(routed, w_gate, preferred_element_type=jnp.float32)
    summed = lax.psum(partial_value.astype(jnp.bfloat16), "exp").astype(jnp.float32)
    acted = jax.nn.silu(summed).astype(jnp.bfloat16)
    produced = jnp.dot(acted, w_down, preferred_element_type=jnp.float32)
    produced = produced.reshape(sources, entries, features)
    returned = lax.all_to_all(
        produced.astype(jnp.bfloat16), "seq", split_axis=0, concat_axis=0, tiled=True
    ).astype(produced.dtype)
    combined = jnp.sum(returned.reshape(experts, group_size, CAP, feature_width), axis=1).reshape(
        experts * CAP, feature_width
    )
    moe_out = jnp.einsum("rt,rd->td", blending, combined, precision=lax.Precision.HIGHEST)
    return (mamba_out, moe_out.astype(jnp.bfloat16))


def solution(mesh):
    return jax.shard_map(
        local,
        mesh=mesh,
        in_specs=(
            P("seq", "exp"),
            P("seq", "exp"),
            P("seq", None),
            P(None, "exp"),
            P("exp"),
            P(None, "exp"),
            P(None, "exp"),
            P("exp"),
            P("exp"),
            P(None, None, "seq"),
            P("seq", "exp"),
            P("exp", None),
            P("seq", None),
            P("exp", "seq"),
            P("seq", "exp"),
        ),
        out_specs=(P("seq", "exp"), P("seq", "exp")),
        check_vma=False,
    )
```

profile of v0, /device:TPU:2, one launch (start us, length us, event | category | flops | bytes accessed | tf_op | source)
XLA Modules:
  0.0 475.2 jit_solution(18132872191936348174)
XLA Ops:
  8.9 3.5 collective-permute-start
  14.1 1.4 compare_select_fusion
  15.5 1.3 slice_bitcast_fusion
  16.9 0.9 maximum_convert_fusion
  18.7 4.2 while.39
  23.9 12.6 %psum.14 = f32[64,8]{0,1:T(8,128)S(1)} all-reduce(f32[64,8]{0,1:T(8,128)S(1)} %fusion.109), channel_id=1, replica_groups=mesh['seq'=64,'exp'=8] {'exp'}, use_global_device_ids=true, to_apply=%region_24.25 | all-reduce | flops 512 | bytes 4096 | tf_op jit(solution)/shard_map/psum | solution.py:116
  38.4 1.3 broadcast_in_dim.47
  39.7 17.2 %all-to-all-start = ((bf16[64,18,512]{2,1,0:T(8,128)(2,1)}), bf16[64,18,512]{2,1,0:T(8,128)(2,1)S(1)}, u32[]{:S(2)}, u32[]{:S(2)}) async-start(bf16[64,18,512]{2,1,0:T(8,128)(2,1)} %bitcast.98), calls=%async_computation | async-start | bytes 3145728 | tf_op jit(solution)/shard_map/all_to_all | solution.py:134
  56.9 1.4 convert_element_type.62
  58.5 75.3 %all-to-all-done = bf16[64,18,512]{2,1,0:T(8,128)(2,1)S(1)} async-done(((bf16[64,18,512]{2,1,0:T(8,128)(2,1)}), bf16[64,18,512]{2,1,0:T(8,128)(2,1)S(1)}, u32[]{:S(2)}, u32[]{:S(2)}) %all-to-all-start) | async-done | bytes 1179680 | tf_op jit(solution)/shard_map/all_to_all | solution.py:134
  133.7 1.2 reshape.657
  134.9 5.0 %convolution_convert_fusion = bf16[1152,1536]{1,0:T(8,128)(2,1)} fusion(bf16[1152,512]{1,0:T(8,128)(2,1)} %reshape.657, bf16[512,1536]{1,0:T(8,128)(2,1)S(1)} %copy-done), kind=kOutput, calls=%fused_computation.255 | convolution fusion | flops 1813708800 | bytes 6291456 | tf_op jit(solution)/shard_map/dot_general | solution.py:137
  140.8 52.6 %all-gather.5.cloned.1.call-done = bf16[1024,1024]{1,0:T(8,128)(2,1)} async-done(((bf16[16,1024]{1,0:T(8,128)(2,1)}), bf16[1024,1024]{1,0:T(8,128)(2,1)}) %all-gather.5.cloned.1.call-update) | async-done | bytes 2097168 | tf_op jit(solution)/shard_map/all_gather | solution.py:18
  193.4 140.1 %all-gather.7.cloned.1.call-done = bf16[1024,1024]{1,0:T(8,128)(2,1)} async-done(((bf16[16,1024]{1,0:T(8,128)(2,1)}), bf16[1024,1024]{1,0:T(8,128)(2,1)}) %all-gather.7.cloned.1.call-update) | async-done | bytes 2097168 | tf_op jit(solution)/shard_map/all_gather | solution.py:18
  333.5 4.6 fusion.93
  338.1 1.3 convert_element_type.73
  339.4 57.4 %all-to-all-start.1 = ((bf16[64,18,512]{2,1,0:T(8,128)(2,1)}), bf16[64,18,512]{2,1,0:T(8,128)(2,1)}, u32[]{:S(2)}, u32[]{:S(2)}) async-start(bf16[64,18,512]{2,1,0:T(8,128)(2,1)} %convert_element_type.73), calls=%async_computation.1 | async-start | bytes 3145728 | tf_op jit(solution)/shard_map/all_to_all | solution.py:142
  396.8 12.9 %while.38 = (s32[]{:T(128)}, f32[16,1024]{1,0:T(8,128)S(1)}, f32[4,16,1024]{2,1,0:T(8,128)S(1)}, f32[4,16,1024]{2,1,0:T(8,128)}, f32[16,1024]{1,0:T(8,128)S(1)},...) while((s32[]{:T(128)}, f32[16,1024]{1,0:T(8,128)S(1)}, ...), condition=%wide.region_21.22_spmd, body=%wide.region_4.21_spmd.sunk | while | flops 2359313 | bytes 1940765 | solution.py:62
  397.0 1.8 constant_dynamic-slice_fusion.114
  400.2 1.8 constant_dynamic-slice_fusion.114
  403.5 1.8 constant_dynamic-slice_fusion.114
  406.7 1.8 constant_dynamic-slice_fusion.114
  410.7 54.4 %all-to-all-done.1 = bf16[64,18,512]{2,1,0:T(8,128)(2,1)} async-done(((bf16[64,18,512]{2,1,0:T(8,128)(2,1)}), bf16[64,18,512]{2,1,0:T(8,128)(2,1)}, u32[]{:S(2)}, u32[]{:S(2)}) %all-to-all-start.1) | async-done | bytes 1179680 | tf_op jit(solution)/shard_map/all_to_all | solution.py:142
  465.1 1.7 convert_reduce_fusion
  (238 shorter events, 17.7 us)
Async XLA Ops:
  8.0 126.9 %copy-start = (bf16[512,1536]{1,0:T(8,128)(2,1)S(1)}, bf16[512,1536]{1,0:T(8,128)(2,1)}, u32[]{:S(2)}) copy-start(bf16[512,1536]{1,0:T(8,128)(2,1)} %param.34) | copy-start | bytes 4718596
  8.0 185.4 %all-gather.5.cloned.1.call-start = ((), (), s32[]{:S(2)}) async-start(), calls=%async_computation.3 | async-start | bytes 2129920 | tf_op jit(solution)/shard_map/all_gather | solution.py:18
  8.9 8.0 %collective-permute-start = (bf16[3,1024]{1,0:T(4,128)(2,1)S(1)}, bf16[3,1024]{1,0:T(4,128)(2,1)S(1)}, u32[]{:S(2)}, u32[]{:S(2)}) collective-permute-start(bf16[3,1024]{1,0:T(4,128)(2,1)S(1)} %slice.515), channel_id=1, source_target_pairs={{0,8},{8,16},{16,24},{24,32},{32,40},{40,48},{48,56},{56,64},{64,7... | collective-permute-start | bytes 18440 | tf_op jit(solution)/shard_map/ppermute | solution.py:12
  18.7 5.0 %copy-start.9 = (s32[64,2]{0,1:T(2,128)S(1)}, s32[64,2]{0,1:T(2,128)}, u32[]{:S(2)}) copy-start(s32[64,2]{0,1:T(2,128)} %param.33) | copy-start | bytes 1540
  18.7 5.1 %copy-start.3 = (bf16[64,512]{1,0:T(8,128)(2,1)S(1)}, bf16[64,512]{1,0:T(8,128)(2,1)}, u32[]{:S(2)}) copy-start(bf16[64,512]{1,0:T(8,128)(2,1)} %param.31) | copy-start | bytes 196612
  18.7 5.0 %copy-start.10 = (bf16[512,8]{0,1:T(8,128)(2,1)S(1)}, bf16[512,8]{0,1:T(8,128)(2,1)}, u32[]{:S(2)}) copy-start(bf16[512,8]{0,1:T(8,128)(2,1)} %param.32) | copy-start | bytes 24580
  22.9 13.7 %copy-start.6 = (f32[16,1024]{1,0:T(8,128)}, f32[16,1024]{1,0:T(8,128)S(1)}, u32[]{:S(2)}) copy-start(f32[16,1024]{1,0:T(8,128)S(1)} %get-tuple-element.127) | copy-start | bytes 196612
  22.9 16.8 %copy-start.1 = (f32[4,16,1024]{2,1,0:T(8,128)}, f32[4,16,1024]{2,1,0:T(8,128)S(1)}, u32[]{:S(2)}) copy-start(f32[4,16,1024]{2,1,0:T(8,128)S(1)} %get-tuple-element.950) | copy-start | bytes 786436
  22.9 16.7 %copy-start.2 = (f32[4,16,1024]{2,1,0:T(8,128)}, f32[4,16,1024]{2,1,0:T(8,128)S(1)}, u32[]{:S(2)}) copy-start(f32[4,16,1024]{2,1,0:T(8,128)S(1)} %get-tuple-element.951) | copy-start | bytes 786436
  39.7 94.1 %all-to-all-start = ((bf16[64,18,512]{2,1,0:T(8,128)(2,1)}), bf16[64,18,512]{2,1,0:T(8,128)(2,1)S(1)}, u32[]{:S(2)}, u32[]{:S(2)}) async-start(bf16[64,18,512]{2,1,0:T(8,128)(2,1)} %bitcast.98), calls=%async_computation | async-start | bytes 3145728 | tf_op jit(solution)/shard_map/all_to_all | solution.py:134
  56.9 276.6 %all-gather.7.cloned.1.call-start = ((), (), s32[]{:S(2)}) async-start(), calls=%async_computation.4 | async-start | bytes 2129920 | tf_op jit(solution)/shard_map/all_gather | solution.py:18
  58.4 275.1 %all-reduce.2.cloned.1.call-start = ((), (), s32[]{:S(2)}) async-start(), calls=%async_computation.2 | async-start | bytes 7077888 | tf_op jit(solution)/shard_map/psum | solution.py:138
  140.0 0.7 copy-start.7
  339.4 125.7 %all-to-all-start.1 = ((bf16[64,18,512]{2,1,0:T(8,128)(2,1)}), bf16[64,18,512]{2,1,0:T(8,128)(2,1)}, u32[]{:S(2)}, u32[]{:S(2)}) async-start(bf16[64,18,512]{2,1,0:T(8,128)(2,1)} %convert_element_type.73), calls=%async_computation.1 | async-start | bytes 3145728 | tf_op jit(solution)/shard_map/all_to_all | solution.py:142
  396.8 13.0 %copy-start.5 = (bf16[64,1024]{1,0:T(8,128)(2,1)S(1)}, bf16[64,1024]{1,0:T(8,128)(2,1)}, u32[]{:S(2)}) copy-start(bf16[64,1024]{1,0:T(8,128)(2,1)} %param.22) | copy-start | bytes 393220
  396.8 13.0 %copy-start.8 = (f32[1024]{0:T(1024)S(1)}, f32[1024]{0:T(1024)}, u32[]{:S(2)}) copy-start(f32[1024]{0:T(1024)} %param.28) | copy-start | bytes 12292
  396.8 13.0 %copy-start.11 = (f32[1024]{0:T(1024)S(1)}, f32[1024]{0:T(1024)}, u32[]{:S(2)}) copy-start(f32[1024]{0:T(1024)} %param.29) | copy-start | bytes 12292
  409.8 57.1 %copy-start.4 = (f32[144,64]{0,1:T(8,128)S(1)}, f32[144,64]{0,1:T(8,128)}, u32[]{:S(2)}) copy-start(f32[144,64]{0,1:T(8,128)} %get-tuple-element.170) | copy-start | bytes 110596
Sparse Core Ops, SparseCore 0:
  23.8 169.5 all-gather.4
  196.3 137.1 all-gather.6
Sparse Core Ops, SparseCore 1:
  140.1 77.3 all-reduce.1
where the time goes:
time: 481 us; the launch traced here: 475 us
  waiting for transfers between devices  322 us (67%)
  starting transfers between devices  78.2 us (16%)
  local copies, waits for them, and re-layouts  18 us (4%)
  between operations  15.8 us (3%)
  other arithmetic  14.6 us (3%)
  blocking collectives  12.6 us (3%)
  matrix products  12.2 us (3%)
    all_gather x2, waiting for transfers between devices, carried_in(): lax.all_gather(a.astype(kind), axis)  193 us
    all_to_all x1, waiting for transfers between devices, local(): lax.all_to_all(outgoing, 'seq', split_axis=0, concat_axis=0, tiled=True)  75.3 us
    all_to_all x1, starting transfers between devices, local(): lax.all_to_all(produced.astype(jnp.bfloat16), 'seq', split_axis=0, concat...  57.4 us
    all_to_all x1, waiting for transfers between devices, local(): lax.all_to_all(produced.astype(jnp.bfloat16), 'seq', split_axis=0, concat...  54.4 us
    all_to_all x1, starting transfers between devices, local(): lax.all_to_all(outgoing, 'seq', split_axis=0, concat_axis=0, tiled=True)  17.2 us
    psum x1, blocking collectives, local(): lax.psum(jnp.dot(hidden, router, preferred_element_type=jnp.float32), 'exp')  12.6 us
  transfers between devices with their start and end apart: 6, of which 4 were waited for; matrix products, arithmetic and copies ran while one was open for 6% of the time, Pallas kernels for 0%

commit v1 on v0

--- a/solution.py
+++ b/solution.py
@@ -4,6 +4,10 @@
 from jax.sharding import PartitionSpec as P
 
 CAP = 18
+
+
+def sizes_shape(message):
+    return jnp.sum(lax.all_gather(message, "exp"), axis=0)
 
 
 def passed_along(value, axis, steps):
@@ -113,7 +117,7 @@
     picks = expert_ids.shape[1]
     feature_width = hidden.shape[1]
     group_size = lax.axis_size("seq") // experts
-    logits = lax.psum(jnp.dot(hidden, router, preferred_element_type=jnp.float32), "exp")
+    logits = sizes_shape(jnp.dot(hidden, router, preferred_element_type=jnp.float32))
     expert_iota = lax.broadcasted_iota(jnp.int32, (1, 1, experts), 2)
     chosen = expert_ids[:, :, None] == expert_iota
     picked = jnp.sum(jnp.where(chosen, logits[:, None, :], 0.0), axis=2)

time: 481 us -> 465 us (0.967)
  waiting for transfers between devices: 322 us -> 305 us
    all_gather x2, waiting for transfers between devices: 193 us -> 173 us  [carried_in(): lax.all_gather(a.astype(kind), axis)]
    all_gather x0 -> x1, blocking collectives: none -> 13.5 us  [sizes_shape(): return jnp.sum(lax.all_gather(message, 'exp'), axis=0)]
    psum x1 -> x0, blocking collectives: 12.6 us -> none  [local(): lax.psum(jnp.dot(hidden, router, preferred_element_type=jnp.float32), 'exp')]
where the time goes in v1:
time: 465 us; the launch traced here: 460 us
  waiting for transfers between devices  305 us (66%)
  starting transfers between devices  78.9 us (17%)
  local copies, waits for them, and re-layouts  18 us (4%)
  between operations  15.8 us (3%)
  other arithmetic  14.6 us (3%)
  blocking collectives  13.5 us (3%)
  matrix products  12.2 us (3%)
    all_gather x2, waiting for transfers between devices, carried_in(): lax.all_gather(a.astype(kind), axis)  173 us
    all_to_all x1, waiting for transfers between devices, local(): lax.all_to_all(outgoing, 'seq', split_axis=0, concat_axis=0, tiled=True)  78.5 us
    all_to_all x1, starting transfers between devices, local(): lax.all_to_all(produced.astype(jnp.bfloat16), 'seq', split_axis=0, concat...  57.4 us
    all_to_all x1, waiting for transfers between devices, local(): lax.all_to_all(produced.astype(jnp.bfloat16), 'seq', split_axis=0, concat...  54.4 us
    all_to_all x1, starting transfers between devices, local(): lax.all_to_all(outgoing, 'seq', split_axis=0, concat_axis=0, tiled=True)  17.9 us
    all_gather x1, blocking collectives, sizes_shape(): return jnp.sum(lax.all_gather(message, 'exp'), axis=0)  13.5 us
  transfers between devices with their start and end apart: 6, of which 4 were waited for; matrix products, arithmetic and copies ran while one was open for 6% of the time, Pallas kernels for 0%

profile of v1, /device:TPU:2, one launch (start us, length us, event | category | flops | bytes accessed | tf_op | source)
XLA Modules:
  0.0 459.7 jit_solution(12764481120808743134)
XLA Ops:
  8.9 3.5 collective-permute-start
  14.1 1.4 compare_select_fusion
  15.5 1.3 slice_bitcast_fusion
  16.9 0.9 maximum_convert_fusion
  18.7 4.2 while.39
  23.9 13.5 %all-gather.3 = f32[8,64,8]{1,2,0:T(8,128)S(1)} all-gather(f32[1,64,8]{1,2,0:T(8,128)S(1)} %convolution_bitcast_fusion), channel_id=4, replica_groups=mesh['seq'=64,'exp'=8] {'exp'}, dimensions={0}, use_global_device_ids=true | all-gather | bytes 18432 | tf_op jit(solution)/shard_map/all_gather | solution.py:10
  39.2 1.3 broadcast_in_dim.47
  40.5 17.9 %all-to-all-start = ((bf16[64,18,512]{2,1,0:T(8,128)(2,1)}), bf16[64,18,512]{2,1,0:T(8,128)(2,1)S(1)}, u32[]{:S(2)}, u32[]{:S(2)}) async-start(bf16[64,18,512]{2,1,0:T(8,128)(2,1)} %bitcast.99), calls=%async_computation | async-start | bytes 3145728 | tf_op jit(solution)/shard_map/all_to_all | solution.py:138
  58.5 1.4 convert_element_type.62
  60.0 78.5 %all-to-all-done = bf16[64,18,512]{2,1,0:T(8,128)(2,1)S(1)} async-done(((bf16[64,18,512]{2,1,0:T(8,128)(2,1)}), bf16[64,18,512]{2,1,0:T(8,128)(2,1)S(1)}, u32[]{:S(2)}, u32[]{:S(2)}) %all-to-all-start) | async-done | bytes 1179680 | tf_op jit(solution)/shard_map/all_to_all | solution.py:138
  138.5 1.2 reshape.657
  139.6 5.0 %convolution_convert_fusion = bf16[1152,1536]{1,0:T(8,128)(2,1)} fusion(bf16[1152,512]{1,0:T(8,128)(2,1)} %reshape.657, bf16[512,1536]{1,0:T(8,128)(2,1)S(1)} %copy-done), kind=kOutput, calls=%fused_computation.255 | convolution fusion | flops 1813708800 | bytes 6291456 | tf_op jit(solution)/shard_map/dot_general | solution.py:141
  145.5 31.4 %all-gather.7.cloned.1.call-done = bf16[1024,1024]{1,0:T(8,128)(2,1)} async-done(((bf16[16,1024]{1,0:T(8,128)(2,1)}), bf16[1024,1024]{1,0:T(8,128)(2,1)}) %all-gather.7.cloned.1.call-update) | async-done | bytes 2097168 | tf_op jit(solution)/shard_map/all_gather | solution.py:22
  176.9 141.1 %all-gather.9.cloned.1.call-done = bf16[1024,1024]{1,0:T(8,128)(2,1)} async-done(((bf16[16,1024]{1,0:T(8,128)(2,1)}), bf16[1024,1024]{1,0:T(8,128)(2,1)}) %all-gather.9.cloned.1.call-update) | async-done | bytes 2097168 | tf_op jit(solution)/shard_map/all_gather | solution.py:22
  318.0 4.5 fusion.93
  322.5 1.3 convert_element_type.73
  323.9 57.4 %all-to-all-start.1 = ((bf16[64,18,512]{2,1,0:T(8,128)(2,1)}), bf16[64,18,512]{2,1,0:T(8,128)(2,1)}, u32[]{:S(2)}, u32[]{:S(2)}) async-start(bf16[64,18,512]{2,1,0:T(8,128)(2,1)} %convert_element_type.73), calls=%async_computation.1 | async-start | bytes 3145728 | tf_op jit(solution)/shard_map/all_to_all | solution.py:146
  381.3 12.9 %while.38 = (s32[]{:T(128)}, f32[16,1024]{1,0:T(8,128)S(1)}, f32[4,16,1024]{2,1,0:T(8,128)S(1)}, f32[4,16,1024]{2,1,0:T(8,128)}, f32[16,1024]{1,0:T(8,128)S(1)},...) while((s32[]{:T(128)}, f32[16,1024]{1,0:T(8,128)S(1)}, ...), condition=%wide.region_21.22_spmd, body=%wide.region_4.21_spmd.sunk | while | flops 2359313 | bytes 1940765 | solution.py:66
  381.5 1.8 constant_dynamic-slice_fusion.114
  384.7 1.8 constant_dynamic-slice_fusion.114
  388.0 1.8 constant_dynamic-slice_fusion.114
  391.2 1.8 constant_dynamic-slice_fusion.114
  395.2 54.4 %all-to-all-done.1 = bf16[64,18,512]{2,1,0:T(8,128)(2,1)} async-done(((bf16[64,18,512]{2,1,0:T(8,128)(2,1)}), bf16[64,18,512]{2,1,0:T(8,128)(2,1)}, u32[]{:S(2)}, u32[]{:S(2)}) %all-to-all-start.1) | async-done | bytes 1179680 | tf_op jit(solution)/shard_map/all_to_all | solution.py:146
  449.6 1.7 convert_reduce_fusion
  (239 shorter events, 17.7 us)
Async XLA Ops:
  8.0 131.7 %copy-start = (bf16[512,1536]{1,0:T(8,128)(2,1)S(1)}, bf16[512,1536]{1,0:T(8,128)(2,1)}, u32[]{:S(2)}) copy-start(bf16[512,1536]{1,0:T(8,128)(2,1)} %param.34) | copy-start | bytes 4718596
  8.0 168.9 %all-gather.7.cloned.1.call-start = ((), (), s32[]{:S(2)}) async-start(), calls=%async_computation.3 | async-start | bytes 2129920 | tf_op jit(solution)/shard_map/all_gather | solution.py:22
  8.9 8.0 %collective-permute-start = (bf16[3,1024]{1,0:T(4,128)(2,1)S(1)}, bf16[3,1024]{1,0:T(4,128)(2,1)S(1)}, u32[]{:S(2)}, u32[]{:S(2)}) collective-permute-start(bf16[3,1024]{1,0:T(4,128)(2,1)S(1)} %slice.515), channel_id=1, source_target_pairs={{0,8},{8,16},{16,24},{24,32},{32,40},{40,48},{48,56},{56,64},{64,7... | collective-permute-start | bytes 18440 | tf_op jit(solution)/shard_map/ppermute | solution.py:16
  18.7 5.0 %copy-start.9 = (s32[64,2]{0,1:T(2,128)S(1)}, s32[64,2]{0,1:T(2,128)}, u32[]{:S(2)}) copy-start(s32[64,2]{0,1:T(2,128)} %param.33) | copy-start | bytes 1540
  18.7 5.1 %copy-start.3 = (bf16[64,512]{1,0:T(8,128)(2,1)S(1)}, bf16[64,512]{1,0:T(8,128)(2,1)}, u32[]{:S(2)}) copy-start(bf16[64,512]{1,0:T(8,128)(2,1)} %param.31) | copy-start | bytes 196612
  18.7 5.0 %copy-start.10 = (bf16[512,8]{0,1:T(8,128)(2,1)S(1)}, bf16[512,8]{0,1:T(8,128)(2,1)}, u32[]{:S(2)}) copy-start(bf16[512,8]{0,1:T(8,128)(2,1)} %param.32) | copy-start | bytes 24580
  22.9 14.5 %copy-start.6 = (f32[16,1024]{1,0:T(8,128)}, f32[16,1024]{1,0:T(8,128)S(1)}, u32[]{:S(2)}) copy-start(f32[16,1024]{1,0:T(8,128)S(1)} %get-tuple-element.127) | copy-start | bytes 196612
  22.9 17.6 %copy-start.1 = (f32[4,16,1024]{2,1,0:T(8,128)}, f32[4,16,1024]{2,1,0:T(8,128)S(1)}, u32[]{:S(2)}) copy-start(f32[4,16,1024]{2,1,0:T(8,128)S(1)} %get-tuple-element.950) | copy-start | bytes 786436
  22.9 17.6 %copy-start.2 = (f32[4,16,1024]{2,1,0:T(8,128)}, f32[4,16,1024]{2,1,0:T(8,128)S(1)}, u32[]{:S(2)}) copy-start(f32[4,16,1024]{2,1,0:T(8,128)S(1)} %get-tuple-element.951) | copy-start | bytes 786436
  40.5 97.9 %all-to-all-start = ((bf16[64,18,512]{2,1,0:T(8,128)(2,1)}), bf16[64,18,512]{2,1,0:T(8,128)(2,1)S(1)}, u32[]{:S(2)}, u32[]{:S(2)}) async-start(bf16[64,18,512]{2,1,0:T(8,128)(2,1)} %bitcast.99), calls=%async_computation | async-start | bytes 3145728 | tf_op jit(solution)/shard_map/all_to_all | solution.py:138
  58.4 259.5 %all-gather.9.cloned.1.call-start = ((), (), s32[]{:S(2)}) async-start(), calls=%async_computation.4 | async-start | bytes 2129920 | tf_op jit(solution)/shard_map/all_gather | solution.py:22
  60.0 258.0 %all-reduce.2.cloned.1.call-start = ((), (), s32[]{:S(2)}) async-start(), calls=%async_computation.2 | async-start | bytes 7077888 | tf_op jit(solution)/shard_map/psum | solution.py:142
  144.7 0.7 copy-start.7
  323.9 125.7 %all-to-all-start.1 = ((bf16[64,18,512]{2,1,0:T(8,128)(2,1)}), bf16[64,18,512]{2,1,0:T(8,128)(2,1)}, u32[]{:S(2)}, u32[]{:S(2)}) async-start(bf16[64,18,512]{2,1,0:T(8,128)(2,1)} %convert_element_type.73), calls=%async_computation.1 | async-start | bytes 3145728 | tf_op jit(solution)/shard_map/all_to_all | solution.py:146
  381.3 13.0 %copy-start.5 = (bf16[64,1024]{1,0:T(8,128)(2,1)S(1)}, bf16[64,1024]{1,0:T(8,128)(2,1)}, u32[]{:S(2)}) copy-start(bf16[64,1024]{1,0:T(8,128)(2,1)} %param.22) | copy-start | bytes 393220
  381.3 13.0 %copy-start.8 = (f32[1024]{0:T(1024)S(1)}, f32[1024]{0:T(1024)}, u32[]{:S(2)}) copy-start(f32[1024]{0:T(1024)} %param.28) | copy-start | bytes 12292
  381.3 13.0 %copy-start.11 = (f32[1024]{0:T(1024)S(1)}, f32[1024]{0:T(1024)}, u32[]{:S(2)}) copy-start(f32[1024]{0:T(1024)} %param.29) | copy-start | bytes 12292
  394.3 57.1 %copy-start.4 = (f32[144,64]{0,1:T(8,128)S(1)}, f32[144,64]{0,1:T(8,128)}, u32[]{:S(2)}) copy-start(f32[144,64]{0,1:T(8,128)} %get-tuple-element.170) | copy-start | bytes 110596
Sparse Core Ops, SparseCore 0:
  23.8 153.0 all-gather.6
  179.8 138.0 all-gather.8
Sparse Core Ops, SparseCore 1:
  144.8 75.7 all-reduce.1
